TPU v7x, 256 devices: a whole 4x4x8 slice. The times are simulated.
256 devices in a mesh: sub: 64 (over y_lo, z, x), blk: 4 (over y_hi, core).
Axes of the slice: x: 4, y: 4 (y_hi: 2, y_lo: 2; y = y_hi * 2 + y_lo), z: 8, core: 2. Of those that a mesh axis runs over, the one named last changes fastest.
Arguments:
- residual: float32 [32, 131072], P(None, ('sub', 'blk')), may hold values from -6 to 6
- fine_inverse: float32 [64, 2560, 2048], P('sub', None, 'blk'), may hold values from -1 to 1.1
- coarse_inverse: float32 [16384, 4, 4096], P('sub', 'blk'), may hold values from -0.5 to 0.5, as said below
- wanted_rows: int32 [64, 2, 256], P('sub'), may hold values from 0 to 2047
- wanted_count: int32 [64, 2], P('sub'), may hold values from 32 to 256, as said below
- aggregate: int32 [131072], P(('sub', 'blk')), may hold values from 0 to 255
Outputs:
- preconditioned: float32 [32, 131072], P(None, ('sub', 'blk'))
Inputs may be any that keep to these rules, and one draw needn't show every extreme that they name: M of the steps is symmetric: coarse_inverse[i, b, s * 64 + q] equals coarse_inverse[s * 256 + b * 64 + q, b2, s2 * 64 + q2] where i = s2 * 256 + b2 * 64 + q2. `wanted_count`: counts vary from side to side; in every draw some subdomain other than the first and last takes exactly 256 rows from one side.
All inputs are finite; a program needn't handle non-finite values.
Results may differ from a plain program's by a relative error of at most 0.000052.
Values sent between devices are 32-bit elements; how exact they have to be, the bound alone decides.
A program may use at most 64 MiB of HBM per device.

v0:
```python
import jax
import jax.numpy as jnp
from jax import lax
from jax.sharding import PartitionSpec as P


def with_halo(cells, sides, width):
    for axis, dim in sides:
        count = lax.axis_size(axis)
        ends = count - 1
        head = lax.slice_in_dim(cells, 0, width, axis=dim)
        tail = lax.slice_in_dim(cells, cells.shape[dim] - width, cells.shape[dim], axis=dim)
        cells = jnp.concatenate(
            [
                lax.ppermute(tail, axis, [(i, (i + 1) % count) for i in range(ends)]),
                cells,
                lax.ppermute(head, axis, [((i + 1) % count, i) for i in range(ends)]),
            ],
            axis=dim,
        )
    return cells


def mask_slots(picked, wanted_total):
    slot_ids = lax.broadcasted_iota(jnp.int32, (1, picked.shape[1]), 1)
    return jnp.where(slot_ids < wanted_total, picked, jnp.zeros_like(picked))


def on_device(residual, fine_inverse, coarse_inverse, wanted_rows, wanted_count, aggregate):
    own_block = lax.all_gather(residual, "blk", axis=1, tiled=True)
    own_len = own_block.shape[1]
    beside = with_halo(own_block, (("sub", 1),), own_len)
    left_raw = jnp.take(beside[:, :own_len], wanted_rows[0, 0], axis=1)
    right_raw = jnp.take(beside[:, 2 * own_len :], wanted_rows[0, 1], axis=1)
    left_halo = mask_slots(left_raw, wanted_count[0, 0])
    right_halo = mask_slots(right_raw, wanted_count[0, 1])
    extended = jnp.concatenate([left_halo, own_block, right_halo], axis=1)
    fine_part = jnp.dot(
        extended,
        fine_inverse[0],
        precision=lax.Precision.HIGHEST,
        preferred_element_type=jnp.float32,
    )
    coarse_table = coarse_inverse[:, 0, :]
    coarse_len = coarse_table.shape[0]
    levels = lax.broadcasted_iota(jnp.int32, (1, coarse_len), 1)
    onehot = (aggregate[:, None] == levels).astype(jnp.float32)
    partial_value = jnp.dot(
        residual, onehot, precision=lax.Precision.HIGHEST, preferred_element_type=jnp.float32
    )
    coarse_share = lax.psum_scatter(partial_value, "blk", scatter_dimension=1, tiled=True)
    partial_solution = lax.dot_general(
        lax.all_gather(coarse_share, "sub", axis=1, tiled=True),
        coarse_table,
        (((1,), (1,)), ((), ())),
        precision=lax.Precision.HIGHEST,
        preferred_element_type=jnp.float32,
    )
    coarse_solution = lax.psum(partial_solution, "blk")
    lifted = lax.dot_general(
        coarse_solution,
        onehot,
        (((1,), (1,)), ((), ())),
        precision=lax.Precision.HIGHEST,
        preferred_element_type=jnp.float32,
    )
    return fine_part + lifted


def solution(mesh):
    in_specs = (
        P(None, ("sub", "blk")),
        P("sub", None, "blk"),
        P("sub", "blk", None),
        P("sub", None, None),
        P("sub", None),
        P(("sub", "blk")),
    )
    out_specs = P(None, ("sub", "blk"))
    return jax.shard_map(
        on_device, mesh=mesh, in_specs=in_specs, out_specs=out_specs, check_vma=False
    )
```

profile of v0, /device:TPU:1, one launch (start us, length us, event | category | flops | bytes accessed | tf_op | source)
XLA Modules:
  0.0 259.5 jit_solution(2096369147131564380)
XLA Ops:
  6.5 0.0 reduce-scatter.4.cloned.1.call-start
  6.5 10.5 %all_gather.6 = f32[32,2048]{1,0:T(8,128)S(1)} all-gather(f32[32,512]{1,0:T(8,128)} %param.8), channel_id=1, replica_groups=mesh['sub'=64,'blk'=4] {'blk'}, dimensions={1}, use_global_device_ids=true | all-gather | bytes 327680 | tf_op jit(solution)/shard_map/all_gather | solution.py:30
  17.1 1.3 collective-permute-start.1
  18.3 4.0 %collective-permute-start = (f32[32,2048]{1,0:T(8,128)S(1)}, f32[32,2048]{1,0:T(8,128)S(1)}, u32[]{:S(2)}, u32[]{:S(2)}) collective-permute-start(f32[32,2048]{1,0:T(8,128)S(1)} %all_gather.6), channel_id=1, source_target_pairs={{0,4},{4,8},{8,12},{12,16},{16,20},{20,24},{24,28},{28,32},{32,36}... | collective-permute-start | bytes 786440 | tf_op jit(solution)/shard_map/ppermute | solution.py:15
  22.4 1.2 convolution_bitcast_fusion
  23.6 0.8 copy.15
  24.3 0.0 reduce-scatter.4.cloned.1.call-update
  24.3 0.8 fusion.17
  25.1 1.3 fusion.18
  26.5 0.6 compare_and_fusion
  27.1 0.7 compare_and_fusion.1
  27.8 31.8 %reduce-scatter.4.cloned.1.call-done = f32[64,32]{1,0:T(8,128)} async-done(((f32[256,32]{1,0:T(8,128)}), f32[64,32]{1,0:T(8,128)}) %reduce-scatter.4.cloned.1.call-update) | async-done | bytes 8208
  59.6 0.8 copy.16
  60.4 133.4 %all-gather = f32[64,64,32]{1,2,0:T(8,128)S(1)} all-gather(f32[1,64,32]{1,2,0:T(8,128)S(1)} %bitcast.29), channel_id=1, replica_groups=mesh['sub'=64,'blk'=4] {'sub'}, dimensions={0}, use_global_device_ids=true | all-gather | bytes 532480 | tf_op jit(solution)/shard_map/all_gather | solution.py:53
  193.8 0.0 copy-start
  193.8 0.6 copy.14
  194.4 0.4 reshape.35
  194.8 7.4 %fusion.2 = f32[32,256]{1,0:T(8,128)S(1)} fusion(f32[4096,32]{0,1:T(8,128)S(1)} %reshape.35, f32[256,1,4096]{2,1,0:T(1,128)} %param.10), kind=kOutput, calls=%fused_computation.4 | convolution fusion | flops 402653184 | bytes 4751360 | tf_op jit(solution)/shard_map/dot_general | solution.py:52
  202.1 41.3 %psum.7 = f32[32,256]{1,0:T(8,128)S(1)} all-reduce(f32[32,256]{1,0:T(8,128)S(1)} %fusion.2), channel_id=1, replica_groups=mesh['sub'=64,'blk'=4] {'blk'}, use_global_device_ids=true, to_apply=%region_1.3 | all-reduce | flops 8192 | bytes 65536 | tf_op jit(solution)/shard_map/psum | solution.py:59
  243.5 0.0 copy-done
  243.5 0.4 fusion.8
  243.9 0.0 collective-permute-done.1
  243.9 0.3 copy.11
  244.3 0.7 gather_fusion.1
  245.0 0.1 bitcast_select_fusion
  245.1 0.1 copy.13
  245.2 0.0 collective-permute-done
  245.2 0.3 copy.10
  245.5 0.7 gather_fusion
  246.3 0.1 bitcast_select_fusion.1
  246.4 0.1 copy.12
  246.5 6.2 %fusion.5 = f32[32,512]{1,0:T(8,128)} fusion(f32[32,512]{1,0:T(8,128)S(1)} %fusion.8, f32[1,2560,512]{2,1,0:T(8,128)} %param.9, f32[32,256]{1,0:T(8,128)S(1)} %copy.13, f32[32,2048]{1,0:T(8,128)S(1)} %all_gather.6, f32[32,256]{1,0:T(8,128)S(1)} %copy.12), kind=kOutput, calls=%fused_computation.7 | convolution fusion | flops 503496704 | bytes 5701632 | tf_op jit(solution)/shard_map/dot_general | solution.py:38
  (4 shorter events, 0.0 us)
Async XLA Ops:
  6.5 53.0 %reduce-scatter.4.cloned.1.call-start = ((), (), s32[]{:S(2)}) async-start(), calls=%async_computation.1 | async-start | bytes 163840
  17.1 226.9 %collective-permute-start.1 = (f32[32,2048]{1,0:T(8,128)S(1)}, f32[32,2048]{1,0:T(8,128)S(1)}, u32[]{:S(2)}, u32[]{:S(2)}) collective-permute-start(f32[32,2048]{1,0:T(8,128)S(1)} %all_gather.6), channel_id=1, source_target_pairs={{4,0},{8,4},{12,8},{16,12},{20,16},{24,20},{28,24},{32,28},{36,32}... | collective-permute-start | bytes 786440 | tf_op jit(solution)/shard_map/ppermute | solution.py:17
  18.3 226.9 %collective-permute-start = (f32[32,2048]{1,0:T(8,128)S(1)}, f32[32,2048]{1,0:T(8,128)S(1)}, u32[]{:S(2)}, u32[]{:S(2)}) collective-permute-start(f32[32,2048]{1,0:T(8,128)S(1)} %all_gather.6), channel_id=1, source_target_pairs={{0,4},{4,8},{8,12},{12,16},{16,20},{20,24},{24,28},{28,32},{32,36}... | collective-permute-start | bytes 786440 | tf_op jit(solution)/shard_map/ppermute | solution.py:15
  193.8 49.7 %copy-start = (s32[512]{0:T(512)S(1)}, s32[512]{0:T(512)}, u32[]{:S(2)}) copy-start(s32[512]{0:T(512)} %param.13) | copy-start | bytes 6148
Sparse Core Ops, SparseCore 0:
  24.5 35.0 reduce-scatter.3
where the time goes:
time: 260 us
  blocking collectives  185 us (71%)
  waiting for transfers between devices  31.8 us (12%)
  matrix products  15.2 us (6%)
  between operations  13.5 us (5%)
  local copies, waits for them, and re-layouts  6.92 us (3%)
  starting transfers between devices  5.29 us (2%)
    all_gather x1, blocking collectives, on_device(): lax.all_gather(coarse_share, 'sub', axis=1, tiled=True)  133 us
    psum x1, blocking collectives, on_device(): coarse_solution = lax.psum(partial_solution, 'blk')  41.3 us
    unnamed x2, waiting for transfers between devices  31.8 us
    all_gather x1, blocking collectives, on_device(): own_block = lax.all_gather(residual, 'blk', axis=1, tiled=True)  10.5 us
    dot_general x1, matrix products, on_device(): lax.dot_general(lax.all_gather(coarse_share, 'sub', axis=1, tiled=True),...  7.38 us
    dot_general x1, matrix products, on_device(): jnp.dot(extended, fine_inverse[0], precision=lax.Precision.HIGHEST, prefe...  6.2 us
  transfers between devices with their start and end apart: 3, of which 1 were waited for; matrix products, arithmetic and copies ran while one was open for 6% of the time, Pallas kernels for 0%

commit v1 on v0

--- a/solution.py
+++ b/solution.py
@@ -2,6 +2,11 @@
 import jax.numpy as jnp
 from jax import lax
 from jax.sharding import PartitionSpec as P
+
+
+def exchange_gather(x, axis, along):
+    stack = jnp.stack([x] * lax.axis_size(axis))
+    return jnp.concatenate(lax.all_to_all(stack, axis, 0, 0), axis=along)
 
 
 def with_halo(cells, sides, width):
@@ -50,7 +55,7 @@
     )
     coarse_share = lax.psum_scatter(partial_value, "blk", scatter_dimension=1, tiled=True)
     partial_solution = lax.dot_general(
-        lax.all_gather(coarse_share, "sub", axis=1, tiled=True),
+        exchange_gather(coarse_share, "sub", 1),
         coarse_table,
         (((1,), (1,)), ((), ())),
         precision=lax.Precision.HIGHEST,

time: 260 us -> 128 us (0.49)
  blocking collectives: 185 us -> 26.5 us
  waiting for transfers between devices: 31.8 us -> 44.6 us
  starting transfers between devices: 5.29 us -> 15.5 us
    all_gather x1 -> x0, blocking collectives: 133 us -> none  [on_device(): lax.all_gather(coarse_share, 'sub', axis=1, tiled=True)]
    psum x1, blocking collectives: 41.3 us -> 15.9 us  [on_device(): coarse_solution = lax.psum(partial_solution, 'blk')]
    all_to_all x0 -> x1, waiting for transfers between devices: none -> 12 us  [exchange_gather(): return jnp.concatenate(lax.all_to_all(stack, axis, 0, 0), axis=along)]
    all_to_all x0 -> x1, starting transfers between devices: none -> 10.2 us  [exchange_gather(): return jnp.concatenate(lax.all_to_all(stack, axis, 0, 0), axis=along)]
  transfers between devices with their start and end apart: 3 -> 4, of which waited for: 1 -> 2; matrix products, arithmetic and copies ran while one was open for 6% -> 8% of each run, Pallas kernels for 0% -> 0%
where the time goes in v1:
time: 128 us
  waiting for transfers between devices  44.6 us (35%)
  blocking collectives  26.5 us (21%)
  starting transfers between devices  15.5 us (12%)
  matrix products  15.2 us (12%)
  between operations  13.6 us (11%)
  local copies, waits for them, and re-layouts  9.38 us (7%)
  other arithmetic  3.39 us (3%)
    unnamed x2, waiting for transfers between devices  32.6 us
    psum x1, blocking collectives, on_device(): coarse_solution = lax.psum(partial_solution, 'blk')  15.9 us
    all_to_all x1, waiting for transfers between devices, exchange_gather(): return jnp.concatenate(lax.all_to_all(stack, axis, 0, 0), axis=along)  12 us
    all_gather x1, blocking collectives, on_device(): own_block = lax.all_gather(residual, 'blk', axis=1, tiled=True)  10.5 us
    all_to_all x1, starting transfers between devices, exchange_gather(): return jnp.concatenate(lax.all_to_all(stack, axis, 0, 0), axis=along)  10.2 us
    dot_general x1, matrix products, on_device(): lax.dot_general(exchange_gather(coarse_share, 'sub', 1), coarse_table, ((...  7.38 us
    dot_general x1, matrix products, on_device(): jnp.dot(extended, fine_inverse[0], precision=lax.Precision.HIGHEST, prefe...  6.21 us
    ppermute x1, starting transfers between devices, with_halo(): lax.ppermute(tail, axis, [(i, (i + 1) % count) for i in range(ends)])  4 us
  transfers between devices with their start and end apart: 4, of which 2 were waited for; matrix products, arithmetic and copies ran while one was open for 8% of the time, Pallas kernels for 0%

profile of v1, /device:TPU:1, one launch (start us, length us, event | category | flops | bytes accessed | tf_op | source)
XLA Modules:
  0.0 128.0 jit_solution(6531148949822479992)
XLA Ops:
  6.5 10.5 %all_gather.3 = f32[32,2048]{1,0:T(8,128)S(1)} all-gather(f32[32,512]{1,0:T(8,128)} %param.8), channel_id=1, replica_groups=mesh['sub'=64,'blk'=4] {'blk'}, dimensions={1}, use_global_device_ids=true | all-gather | bytes 327680 | tf_op jit(solution)/shard_map/all_gather | solution.py:35
  17.1 1.3 %collective-permute-start.1 = (f32[32,2048]{1,0:T(8,128)S(1)}, f32[32,2048]{1,0:T(8,128)S(1)}, u32[]{:S(2)}, u32[]{:S(2)}) collective-permute-start(f32[32,2048]{1,0:T(8,128)S(1)} %all_gather.3), channel_id=1, source_target_pairs={{4,0},{8,4},{12,8},{16,12},{20,16},{24,20},{28,24},{32,28},{36,32}... | collective-permute-start | bytes 786440 | tf_op jit(solution)/shard_map/ppermute | solution.py:22
  18.3 4.0 %collective-permute-start = (f32[32,2048]{1,0:T(8,128)S(1)}, f32[32,2048]{1,0:T(8,128)S(1)}, u32[]{:S(2)}, u32[]{:S(2)}) collective-permute-start(f32[32,2048]{1,0:T(8,128)S(1)} %all_gather.3), channel_id=1, source_target_pairs={{0,4},{4,8},{8,12},{12,16},{16,20},{20,24},{24,28},{28,32},{32,36}... | collective-permute-start | bytes 786440 | tf_op jit(solution)/shard_map/ppermute | solution.py:20
  22.4 1.2 convolution_bitcast_fusion
  23.6 0.7 copy.14
  24.3 0.8 fusion.17
  25.1 1.3 %fusion.18 = (s32[1,1]{1,0:T(1,128)}, s32[1,1]{1,0:T(1,128)}) fusion(s32[1,2]{1,0:T(1,128)} %param.12), kind=kLoop, calls=%fused_computation.30 | loop fusion | bytes 16 | tf_op jit(solution)/shard_map/slice | solution.py:40
  26.4 0.6 compare_and_fusion
  27.0 32.6 %reduce-scatter.4.cloned.1.call-done = f32[64,32]{1,0:T(8,128)} async-done(((f32[256,32]{1,0:T(8,128)}), f32[64,32]{1,0:T(8,128)}) %reduce-scatter.4.cloned.1.call-update) | async-done | bytes 8208
  59.6 0.8 copy.15
  60.4 0.1 stack.2
  60.5 1.4 %reshape.50 = f32[64,1,2048]{2,1,0:T(1,128)} reshape(f32[64,32,64]{2,1,0:T(8,128)S(1)} %stack.2) | data formatting | bytes 1048576
  62.0 10.2 %all-to-all-start = ((f32[64,1,2048]{2,1,0:T(1,128)}), f32[64,1,2048]{2,1,0:T(1,128)S(1)}, u32[]{:S(2)}, u32[]{:S(2)}) async-start(f32[64,1,2048]{2,1,0:T(1,128)} %reshape.50), calls=%async_computation | async-start | bytes 1048576 | tf_op jit(solution)/shard_map/all_to_all | solution.py:9
  72.1 0.7 compare_and_fusion.1
  72.8 0.3 copy.10
  73.2 0.7 gather_fusion.1
  73.9 0.1 bitcast_select_fusion
  74.1 0.1 copy.12
  74.1 0.3 copy.9
  74.5 0.7 gather_fusion
  75.2 0.1 bitcast_select_fusion.1
  75.4 0.1 copy.11
  75.4 12.0 %all-to-all-done = f32[64,1,2048]{2,1,0:T(1,128)S(1)} async-done(((f32[64,1,2048]{2,1,0:T(1,128)}), f32[64,1,2048]{2,1,0:T(1,128)S(1)}, u32[]{:S(2)}, u32[]{:S(2)}) %all-to-all-start) | async-done | bytes 524320 | tf_op jit(solution)/shard_map/all_to_all | solution.py:9
  87.4 0.5 broadcast.44
  87.9 1.9 %reduce = f32[64,2048]{1,0:T(8,128)S(1)} reduce(f32[64,1,2048]{2,1,0:T(1,128)S(1)} %all-to-all-done, f32[]{:T(128)} %broadcast.44), dimensions={1}, to_apply=%all_to_all.3.reduce_sub_computation | reduce | bytes 1048580 | tf_op jit(solution)/shard_map/all_to_all | solution.py:9
  89.8 0.4 reshape.51
  90.2 0.6 copy.13
  90.8 0.4 reshape.25
  91.2 7.4 %fusion.2 = f32[32,256]{1,0:T(8,128)S(1)} fusion(f32[32,4096]{1,0:T(8,128)S(1)} %reshape.25, f32[256,1,4096]{2,1,0:T(1,128)} %param.10), kind=kOutput, calls=%fused_computation.4 | convolution fusion | flops 402653184 | bytes 4751360 | tf_op jit(solution)/shard_map/dot_general | solution.py:57
  98.6 15.9 %psum.7 = f32[32,256]{1,0:T(8,128)S(1)} all-reduce(f32[32,256]{1,0:T(8,128)S(1)} %fusion.2), channel_id=1, replica_groups=mesh['sub'=64,'blk'=4] {'blk'}, use_global_device_ids=true, to_apply=%region_1.3 | all-reduce | flops 8192 | bytes 65536 | tf_op jit(solution)/shard_map/psum | solution.py:64
  114.6 0.4 fusion.8
  114.9 6.2 %fusion.5 = f32[32,512]{1,0:T(8,128)} fusion(f32[32,512]{1,0:T(8,128)S(1)} %fusion.8, f32[1,2560,512]{2,1,0:T(8,128)} %param.9, f32[32,256]{1,0:T(8,128)S(1)} %copy.12, f32[32,2048]{1,0:T(8,128)S(1)} %all_gather.3, f32[32,256]{1,0:T(8,128)S(1)} %copy.11), kind=kOutput, calls=%fused_computation.7 | convolution fusion | flops 503496704 | bytes 5701632 | tf_op jit(solution)/shard_map/dot_general | solution.py:43
  (10 shorter events, 0.1 us)
Async XLA Ops:
  6.5 53.0 %reduce-scatter.4.cloned.1.call-start = ((), (), s32[]{:S(2)}) async-start(), calls=%async_computation.2 | async-start | bytes 163840
  17.1 55.8 %collective-permute-start.1 = (f32[32,2048]{1,0:T(8,128)S(1)}, f32[32,2048]{1,0:T(8,128)S(1)}, u32[]{:S(2)}, u32[]{:S(2)}) collective-permute-start(f32[32,2048]{1,0:T(8,128)S(1)} %all_gather.3), channel_id=1, source_target_pairs={{4,0},{8,4},{12,8},{16,12},{20,16},{24,20},{28,24},{32,28},{36,32}... | collective-permute-start | bytes 786440 | tf_op jit(solution)/shard_map/ppermute | solution.py:22
  18.3 55.8 %collective-permute-start = (f32[32,2048]{1,0:T(8,128)S(1)}, f32[32,2048]{1,0:T(8,128)S(1)}, u32[]{:S(2)}, u32[]{:S(2)}) collective-permute-start(f32[32,2048]{1,0:T(8,128)S(1)} %all_gather.3), channel_id=1, source_target_pairs={{0,4},{4,8},{8,12},{12,16},{16,20},{20,24},{24,28},{28,32},{32,36}... | collective-permute-start | bytes 786440 | tf_op jit(solution)/shard_map/ppermute | solution.py:20
  62.0 25.4 %all-to-all-start = ((f32[64,1,2048]{2,1,0:T(1,128)}), f32[64,1,2048]{2,1,0:T(1,128)S(1)}, u32[]{:S(2)}, u32[]{:S(2)}) async-start(f32[64,1,2048]{2,1,0:T(1,128)} %reshape.50), calls=%async_computation | async-start | bytes 1048576 | tf_op jit(solution)/shard_map/all_to_all | solution.py:9
  90.2 24.3 %copy-start = (s32[512]{0:T(512)S(1)}, s32[512]{0:T(512)}, u32[]{:S(2)}) copy-start(s32[512]{0:T(512)} %param.13) | copy-start | bytes 6148
Sparse Core Ops, SparseCore 0:
  24.4 35.0 reduce-scatter.3

commit v2 on v0

--- a/solution.py
+++ b/solution.py
@@ -2,6 +2,11 @@
 import jax.numpy as jnp
 from jax import lax
 from jax.sharding import PartitionSpec as P
+
+
+def gather_and_add(x, axis):
+    blocks = lax.all_gather(x, axis)
+    return jnp.sum(blocks, axis=0)
 
 
 def with_halo(cells, sides, width):
@@ -56,7 +61,7 @@
         precision=lax.Precision.HIGHEST,
         preferred_element_type=jnp.float32,
     )
-    coarse_solution = lax.psum(partial_solution, "blk")
+    coarse_solution = gather_and_add(partial_solution, "blk")
     lifted = lax.dot_general(
         coarse_solution,
         onehot,

time: 260 us -> 254 us (0.977)
  blocking collectives: 185 us -> 180 us
    psum x1 -> x0, blocking collectives: 41.3 us -> none  [on_device(): coarse_solution = lax.psum(partial_solution, 'blk')]
    all_gather x0 -> x1, blocking collectives: none -> 35.6 us  [gather_and_add(): blocks = lax.all_gather(x, axis)]
where the time goes in v2:
time: 254 us
  blocking collectives  180 us (71%)
  waiting for transfers between devices  31.8 us (13%)
  matrix products  15.2 us (6%)
  between operations  13.5 us (5%)
  local copies, waits for them, and re-layouts  6.92 us (3%)
  starting transfers between devices  5.29 us (2%)
    all_gather x1, blocking collectives, on_device(): lax.all_gather(coarse_share, 'sub', axis=1, tiled=True)  133 us
    all_gather x1, blocking collectives, gather_and_add(): blocks = lax.all_gather(x, axis)  35.6 us
    unnamed x2, waiting for transfers between devices  31.8 us
    all_gather x1, blocking collectives, on_device(): own_block = lax.all_gather(residual, 'blk', axis=1, tiled=True)  10.5 us
    dot_general x1, matrix products, on_device(): lax.dot_general(lax.all_gather(coarse_share, 'sub', axis=1, tiled=True),...  7.38 us
    dot_general x1, matrix products, on_device(): jnp.dot(extended, fine_inverse[0], precision=lax.Precision.HIGHEST, prefe...  6.2 us
  transfers between devices with their start and end apart: 3, of which 1 were waited for; matrix products, arithmetic and copies ran while one was open for 6% of the time, Pallas kernels for 0%

profile of v2, /device:TPU:1, one launch (start us, length us, event | category | flops | bytes accessed | tf_op | source)
XLA Modules:
  0.0 253.8 jit_solution(8287578799915773218)
XLA Ops:
  6.5 0.0 reduce-scatter.4.cloned.1.call-start
  6.5 10.5 %all_gather.12 = f32[32,2048]{1,0:T(8,128)S(1)} all-gather(f32[32,512]{1,0:T(8,128)} %param.8), channel_id=1, replica_groups=mesh['sub'=64,'blk'=4] {'blk'}, dimensions={1}, use_global_device_ids=true | all-gather | bytes 327680 | tf_op jit(solution)/shard_map/all_gather | solution.py:35
  17.1 1.3 collective-permute-start.1
  18.3 4.0 %collective-permute-start = (f32[32,2048]{1,0:T(8,128)S(1)}, f32[32,2048]{1,0:T(8,128)S(1)}, u32[]{:S(2)}, u32[]{:S(2)}) collective-permute-start(f32[32,2048]{1,0:T(8,128)S(1)} %all_gather.12), channel_id=1, source_target_pairs={{0,4},{4,8},{8,12},{12,16},{16,20},{20,24},{24,28},{28,32},{32,36}... | collective-permute-start | bytes 786440 | tf_op jit(solution)/shard_map/ppermute | solution.py:20
  22.4 1.2 convolution_bitcast_fusion
  23.6 0.8 copy.15
  24.3 0.0 reduce-scatter.4.cloned.1.call-update
  24.3 0.8 fusion.17
  25.1 1.3 fusion.18
  26.5 0.6 compare_and_fusion
  27.1 0.7 compare_and_fusion.1
  27.8 31.8 %reduce-scatter.4.cloned.1.call-done = f32[64,32]{1,0:T(8,128)} async-done(((f32[256,32]{1,0:T(8,128)}), f32[64,32]{1,0:T(8,128)}) %reduce-scatter.4.cloned.1.call-update) | async-done | bytes 8208
  59.6 0.8 copy.16
  60.4 133.4 %all-gather.1 = f32[64,64,32]{1,2,0:T(8,128)S(1)} all-gather(f32[1,64,32]{1,2,0:T(8,128)S(1)} %bitcast.31), channel_id=1, replica_groups=mesh['sub'=64,'blk'=4] {'sub'}, dimensions={0}, use_global_device_ids=true | all-gather | bytes 532480 | tf_op jit(solution)/shard_map/all_gather | solution.py:58
  193.8 0.0 copy-start
  193.8 0.6 copy.14
  194.4 0.4 reshape.36
  194.8 7.4 %fusion.2 = f32[32,256]{1,0:T(8,128)S(1)} fusion(f32[4096,32]{0,1:T(8,128)S(1)} %reshape.36, f32[256,1,4096]{2,1,0:T(1,128)} %param.10), kind=kOutput, calls=%fused_computation.4 | convolution fusion | flops 402653184 | bytes 4751360 | tf_op jit(solution)/shard_map/dot_general | solution.py:57
  202.1 35.6 %all-gather = f32[128,256]{1,0:T(8,128)S(1)} all-gather(f32[32,256]{1,0:T(8,128)S(1)} %fusion.2), channel_id=2, replica_groups=mesh['sub'=64,'blk'=4] {'blk'}, dimensions={0}, use_global_device_ids=true | all-gather | bytes 163840 | tf_op jit(solution)/shard_map/all_gather | solution.py:8
  237.8 0.0 copy-done
  237.8 0.4 fusion.8
  238.2 0.0 collective-permute-done.1
  238.2 0.3 copy.11
  238.5 0.7 gather_fusion.1
  239.3 0.1 bitcast_select_fusion
  239.4 0.1 copy.13
  239.5 0.0 collective-permute-done
  239.5 0.3 copy.10
  239.8 0.7 gather_fusion
  240.6 0.1 bitcast_select_fusion.1
  240.7 0.1 copy.12
  240.8 6.2 %fusion.5 = f32[32,512]{1,0:T(8,128)} fusion(f32[32,512]{1,0:T(8,128)S(1)} %fusion.8, f32[1,2560,512]{2,1,0:T(8,128)} %param.9, f32[32,256]{1,0:T(8,128)S(1)} %copy.13, f32[32,2048]{1,0:T(8,128)S(1)} %all_gather.12, f32[32,256]{1,0:T(8,128)S(1)} %copy.12), kind=kOutput, calls=%fused_computation.7 | convolution fusion | flops 503496704 | bytes 5701632 | tf_op jit(solution)/shard_map/dot_general | solution.py:43
  (5 shorter events, 0.0 us)
Async XLA Ops:
  6.5 53.0 %reduce-scatter.4.cloned.1.call-start = ((), (), s32[]{:S(2)}) async-start(), calls=%async_computation.1 | async-start | bytes 163840
  17.1 221.1 %collective-permute-start.1 = (f32[32,2048]{1,0:T(8,128)S(1)}, f32[32,2048]{1,0:T(8,128)S(1)}, u32[]{:S(2)}, u32[]{:S(2)}) collective-permute-start(f32[32,2048]{1,0:T(8,128)S(1)} %all_gather.12), channel_id=1, source_target_pairs={{4,0},{8,4},{12,8},{16,12},{20,16},{24,20},{28,24},{32,28},{36,32}... | collective-permute-start | bytes 786440 | tf_op jit(solution)/shard_map/ppermute | solution.py:22
  18.3 221.1 %collective-permute-start = (f32[32,2048]{1,0:T(8,128)S(1)}, f32[32,2048]{1,0:T(8,128)S(1)}, u32[]{:S(2)}, u32[]{:S(2)}) collective-permute-start(f32[32,2048]{1,0:T(8,128)S(1)} %all_gather.12), channel_id=1, source_target_pairs={{0,4},{4,8},{8,12},{12,16},{16,20},{20,24},{24,28},{28,32},{32,36}... | collective-permute-start | bytes 786440 | tf_op jit(solution)/shard_map/ppermute | solution.py:20
  193.8 44.0 %copy-start = (s32[512]{0:T(512)S(1)}, s32[512]{0:T(512)}, u32[]{:S(2)}) copy-start(s32[512]{0:T(512)} %param.13) | copy-start | bytes 6148
Sparse Core Ops, SparseCore 0:
  24.5 35.0 reduce-scatter.3
